TPU v7x, 256 devices: a whole 4x4x8 slice. The times are simulated.
256 devices in a mesh: dp: 32 (over z, y_hi, core), owner: 8 (over y_lo, x).
Axes of the slice: x: 4, y: 4 (y_hi: 2, y_lo: 2; y = y_hi * 2 + y_lo), z: 8, core: 2. Of those that a mesh axis runs over, the one named last changes fastest.
Arguments:
- hidden: bfloat16 [4096, 4096], P('dp'), may hold values from -6 to 6
- norm_gain: float32 [4096], replicated, may hold values from 0.3 to 3
- cotangent: bfloat16 [4096, 6144], P('dp'), may hold values from -30 to 30
Outputs:
- update: bfloat16 [6144, 4096], P('dp', 'owner')
All inputs are finite; a program needn't handle non-finite values. Where the computation divides by a largest or mean magnitude, that divisor is 1e-20 or more.
Results may differ from a plain program's by a relative error of at most 0.014.
Values may be sent and summed in bfloat16 or wider, within the bound.
No kernel may reach another device: no remote copies, remote signals or barrier semaphores. Data moves between devices by JAX's collectives and lax.ppermute only.
A program may use at most 128 MiB of HBM per device.

v0:
```python
import functools
import jax
import jax.numpy as jnp
from jax import lax
from jax.sharding import Mesh
from jax.sharding import PartitionSpec as P

TILE = 1024
OWNER = ("owner_0", "owner_1")
DP = ("dp_0", "dp_1", "dp_2")
DP_OWNER = ("dp_0", "dp_1", "dp_2", "owner_0", "owner_1")
DAMPING = 0.1


def padded_to(lines, length):
    spare = -lines.shape[0] % length
    if not spare:
        return lines
    return jnp.concatenate([lines, jnp.zeros((spare, *lines.shape[1:]), lines.dtype)])


def sum_in_two_steps(shard, axis):
    lines = shard.reshape(-1, *shard.shape[1:][-1:])
    own = lax.psum_scatter(
        padded_to(lines, lax.axis_size(axis)), axis, scatter_dimension=0, tiled=True
    )
    whole = lax.all_gather(own, axis).reshape(-1, *lines.shape[1:])
    return lax.slice_in_dim(whole, 0, len(lines)).reshape(shard.shape)


def over_axes(shard, axes):
    return functools.reduce(lax.psum, axes, shard)


def shards(hidden, norm_gain, cotangent):
    owners = lax.axis_size(OWNER)
    position = lax.axis_index(OWNER)
    groups = lax.axis_size(DP)
    tokens_here = hidden.shape[0]
    width = hidden.shape[1]
    out_width = cotangent.shape[1]
    blocks_all = (width + out_width) // TILE
    slots = (blocks_all + owners - 1) // owners
    states = hidden.astype(jnp.float32)
    normed = (
        states * lax.rsqrt(jnp.mean(states * states, axis=1, keepdims=True) + 1e-05) * norm_gain
    ).astype(jnp.bfloat16)
    source = jnp.concatenate([normed, cotangent], axis=1)
    columns = []
    for slot in range(slots):
        block = jnp.minimum(position + slot * owners, blocks_all - 1)
        columns.append(lax.dynamic_slice_in_dim(source, block * TILE, TILE, 1))
    pieces = jnp.stack(columns)
    partial_value = jnp.einsum("stk,stl->skl", pieces, pieces, preferred_element_type=jnp.float32)
    identity = jnp.eye(TILE, dtype=jnp.float32)
    factor = sum_in_two_steps(partial_value, DP)
    matrix = factor / (tokens_here * groups) + DAMPING * identity
    scale = 1.0 / jnp.max(jnp.sum(jnp.abs(matrix), axis=2), axis=1)
    first = 2.0 * scale[:, None, None] * identity - (scale * scale)[:, None, None] * matrix
    first_low = first.astype(jnp.bfloat16)
    matrix_low = matrix.astype(jnp.bfloat16)
    product = jnp.einsum(
        "skl,slm->skm", first_low, matrix_low, preferred_element_type=jnp.float32
    ).astype(jnp.bfloat16)
    inverse = (
        2.0 * first
        - jnp.einsum("skl,slm->skm", product, first_low, preferred_element_type=jnp.float32)
    ).astype(jnp.bfloat16)
    precond = jnp.einsum(
        "stk,skl->stl", pieces, inverse, preferred_element_type=jnp.float32
    ).astype(jnp.bfloat16)
    gathered = lax.all_gather(precond[:, None], OWNER, axis=1, tiled=True)
    ordered = gathered.reshape(slots * owners, tokens_here, TILE)[:blocks_all]
    inputs_side = width // TILE
    pre_in = jnp.transpose(ordered[:inputs_side], (1, 0, 2)).reshape(tokens_here, width)
    pre_out = jnp.transpose(ordered[inputs_side:], (1, 0, 2)).reshape(tokens_here, out_width)
    own_rows = width // owners
    mine_in = lax.dynamic_slice_in_dim(pre_in, position * own_rows, own_rows, 1)
    summed = lax.psum_scatter(
        jnp.einsum("tk,tl->kl", pre_out, mine_in, preferred_element_type=jnp.float32).astype(
            jnp.bfloat16
        ),
        DP,
        scatter_dimension=0,
        tiled=True,
    ).astype(jnp.float32)
    squares = over_axes(jnp.sum(summed * summed), DP_OWNER)
    return (summed * lax.rsqrt(squares / (width * out_width) + 1e-06)).astype(jnp.bfloat16)


def solution(mesh):
    split = Mesh(
        mesh.devices.reshape(8, 2, 2, 2, 4), ("dp_0", "dp_1", "dp_2", "owner_0", "owner_1")
    )
    return jax.shard_map(
        shards,
        mesh=split,
        in_specs=(P(DP, None), P(), P(DP, None)),
        out_specs=P(DP, OWNER),
        check_vma=False,
    )
```

profile of v0, /device:TPU:8, one launch (start us, length us, event | category | flops | bytes accessed | tf_op | source)
XLA Modules:
  0.0 577.2 jit_solution(10745259062472830327)
XLA Ops:
  6.5 0.0 reduce-scatter.3.cloned.1.call-start
  6.5 1.5 fusion.10
  8.1 1.6 fusion.12
  9.6 1.3 fusion.19
  10.9 4.5 fusion.16
  15.4 0.0 reduce-scatter.3.cloned.1.call-update
  15.4 0.0 all-gather.5.cloned.1.call-start
  15.5 156.2 %reduce-scatter.3.cloned.1.call-done = f32[64,1024]{1,0:T(8,128)} async-done(((f32[2048,1024]{1,0:T(8,128)}), f32[64,1024]{1,0:T(8,128)}) %reduce-scatter.3.cloned.1.call-update) | async-done | bytes 262160 | tf_op jit(solution)/shard_map/reduce_scatter | solution.py:24
  171.7 0.0 all-gather.5.cloned.1.call-update
  171.7 0.0 all-gather.7.cloned.1.call-start
  171.7 2.4 fusion.6
  174.2 2.5 fusion.5
  176.7 97.3 %all-gather.5.cloned.1.call-done = f32[2048,1024]{1,0:T(8,128)} async-done(((f32[64,1024]{1,0:T(8,128)}), f32[2048,1024]{1,0:T(8,128)}) %all-gather.5.cloned.1.call-update) | async-done | bytes 8388624 | tf_op jit(solution)/shard_map/all_gather | solution.py:27
  273.9 0.0 copy-start.1
  273.9 5.4 broadcast_multiply_fusion
  279.4 0.0 copy-start
  279.4 0.0 copy-done.1
  279.4 4.7 add.64
  284.1 1.0 copy-done
  285.1 4.3 abs_reduce_fusion
  289.4 0.1 reduce_max.10
  289.5 0.1 reduce_max.14
  289.6 0.1 reduce_max.18
  289.7 24.7 %fusion.2 = f32[2,1024,1024]{2,1,0:T(8,128)} fusion(f32[2,1024,1024]{2,1,0:T(8,128)} %bitcast.17, f32[1024,1024]{1,0:T(8,128)} %fusion.6, f32[2]{0:T(128)S(1)} %mul.104, f32[1024,1024]{1,0:T(8,128)} %fusion.5, f32[2]{0:T(128)S(1)} %get-tuple-element.5), kind=kOutput, calls=%fused_computation.8 | convolution fusion | flops 8617197568 | bytes 25165840 | tf_op jit(solution)/shard_map/skl,slm->skm/dot_general | solution.py:67
  314.5 10.4 %fusion.13 = bf16[2,128,1024]{2,1,0:T(8,128)(2,1)} fusion(f32[2,1024,1024]{2,1,0:T(8,128)} %fusion.2, f32[2,1024,1024]{2,1,0:T(8,128)} %bitcast.18, f32[2]{0:T(128)S(1)} %mul.104, f32[1024,1024]{1,0:T(8,128)} %fusion.5, f32[2]{0:T(128)S(1)} %get-tuple-element.5, f32[1024,1024]{1,0:T(8,128)} %fusion.6, bf16[1,128,1024]{2,1,0:T(8,128)(2,1)S(1)} %get-tuple-element.8, ...), kind=kOutput, calls=%fused_computation.24 | convolution fusion | flops 552075264 | bytes 26214416 | tf_op jit(solution)/shard_map/stk,skl->stl/dot_general | solution.py:69
  324.8 0.0 all-gather.7.cloned.1.call-update
  324.9 0.2 reduce-scatter.5.cloned.1.call-start
  325.1 51.5 %all-gather.7.cloned.1.call-done = bf16[2,1024,1024]{2,1,0:T(8,128)(2,1)} async-done(((bf16[2,128,1024]{2,1,0:T(8,128)(2,1)}), bf16[2,1024,1024]{2,1,0:T(8,128)(2,1)}) %all-gather.7.cloned.1.call-update) | async-done | bytes 4194320 | tf_op jit(solution)/shard_map/all_gather | solution.py:72
  376.6 1.5 slice.11
  378.1 2.3 slice.12
  380.4 0.9 copy.12
  381.3 1.6 copy.13
  382.9 4.5 convolution_convert_fusion
  387.4 0.0 reduce-scatter.5.cloned.1.call-update
  387.4 135.9 %reduce-scatter.5.cloned.1.call-done = bf16[192,512]{1,0:T(8,128)(2,1)} async-done(((bf16[6144,512]{1,0:T(8,128)(2,1)}), bf16[192,512]{1,0:T(8,128)(2,1)}) %reduce-scatter.5.cloned.1.call-update) | async-done | bytes 196624 | tf_op jit(solution)/shard_map/reduce_scatter | solution.py:79
  523.3 1.6 fusion.14
  524.9 16.6 %psum.35 = f32[]{:T(128)} all-reduce(f32[]{:T(128)} %fusion.14), channel_id=1, replica_groups=mesh['dp_0'=8,'dp_1'=2,'dp_2'=2,'owner_0'=2,'owner_1'=4] {'dp_0'}, use_global_device_ids=true, to_apply=%region_7.0 | all-reduce | flops 1 | bytes 8 | tf_op jit(solution)/shard_map/psum | solution.py:32
  541.5 7.1 %psum.36 = f32[]{:T(128)} all-reduce(f32[]{:T(128)} %psum.35), channel_id=1, replica_groups=mesh['dp_0'=8,'dp_1'=2,'dp_2'=2,'owner_0'=2,'owner_1'=4] {'dp_1'}, use_global_device_ids=true, to_apply=%region_8.0 | all-reduce | flops 1 | bytes 8 | tf_op jit(solution)/shard_map/psum | solution.py:32
  548.6 3.1 psum.37
  551.7 5.6 psum.38
  557.2 11.1 %psum.39 = f32[]{:T(128)} all-reduce(f32[]{:T(128)} %psum.38), channel_id=1, replica_groups=mesh['dp_0'=8,'dp_1'=2,'dp_2'=2,'owner_0'=2,'owner_1'=4] {'owner_1'}, use_global_device_ids=true, to_apply=%region_11.12 | all-reduce | flops 1 | bytes 8 | tf_op jit(solution)/shard_map/psum | solution.py:32
  569.0 1.6 fusion.15
  (3 shorter events, 0.0 us)
Async XLA Ops:
  6.5 165.1 %reduce-scatter.3.cloned.1.call-start = ((), (), s32[]{:S(2)}) async-start(), calls=%async_computation.2 | async-start | bytes 8650752 | tf_op jit(solution)/shard_map/reduce_scatter | solution.py:24
  15.4 258.5 %all-gather.5.cloned.1.call-start = ((), (), s32[]{:S(2)}) async-start(), calls=%async_computation.4 | async-start | bytes 8650752 | tf_op jit(solution)/shard_map/all_gather | solution.py:27
  171.7 204.9 %all-gather.7.cloned.1.call-start = ((), (), s32[]{:S(2)}) async-start(), calls=%async_computation.5 | async-start | bytes 4718592 | tf_op jit(solution)/shard_map/all_gather | solution.py:72
  273.9 5.5 copy-start.1
  279.4 5.7 copy-start
  324.9 198.4 %reduce-scatter.5.cloned.1.call-start = ((), (), s32[]{:S(2)}) async-start(), calls=%async_computation.3 | async-start | bytes 6488064 | tf_op jit(solution)/shard_map/reduce_scatter | solution.py:79
Sparse Core Ops, SparseCore 0:
  15.6 156.0 reduce-scatter.2
  174.5 99.4 all-gather.4
  325.0 51.5 all-gather.6
  387.5 135.7 reduce-scatter.4
where the time goes:
time: 578 us; the launch traced here: 577 us
  waiting for transfers between devices  441 us (76%)
  matrix products  44.1 us (8%)
  blocking collectives  43.4 us (8%)
  other arithmetic  22.5 us (4%)
  between operations  13.9 us (2%)
  local copies, waits for them, and re-layouts  12.1 us (2%)
    reduce_scatter x1, waiting for transfers between devices, sum_in_two_steps(): lax.psum_scatter(padded_to(lines, lax.axis_size(axis)), axis, scatter_dim...  156 us
    reduce_scatter x1, waiting for transfers between devices, shards(): lax.psum_scatter(jnp.einsum('tk,tl->kl', pre_out, mine_in, preferred_elem...  136 us
    all_gather x1, waiting for transfers between devices, sum_in_two_steps(): whole = lax.all_gather(own, axis).reshape(-1, *lines.shape[1:])  97.3 us
    all_gather x1, waiting for transfers between devices, shards(): gathered = lax.all_gather(precond[:, None], OWNER, axis=1, tiled=True)  51.5 us
    psum x5, blocking collectives, over_axes(): return functools.reduce(lax.psum, axes, shard)  43.4 us
    dot_general x1, matrix products, shards(): jnp.einsum('skl,slm->skm', product, first_low, preferred_element_type=jnp...  24.7 us
  transfers between devices with their start and end apart: 4, of which 4 were waited for; matrix products, arithmetic and copies ran while one was open for 1% of the time, Pallas kernels for 0%

commit v1 on v0

--- a/solution.py
+++ b/solution.py
@@ -69,7 +69,9 @@
     precond = jnp.einsum(
         "stk,skl->stl", pieces, inverse, preferred_element_type=jnp.float32
     ).astype(jnp.bfloat16)
-    gathered = lax.all_gather(precond[:, None], OWNER, axis=1, tiled=True)
+    gathered = jnp.concatenate(
+        lax.all_to_all(jnp.stack([precond[:, None]] * lax.axis_size(OWNER)), OWNER, 0, 0), axis=1
+    )
     ordered = gathered.reshape(slots * owners, tokens_here, TILE)[:blocks_all]
     inputs_side = width // TILE
     pre_in = jnp.transpose(ordered[:inputs_side], (1, 0, 2)).reshape(tokens_here, width)

time: 578 us -> 592 us (1.024)
  waiting for transfers between devices: 441 us -> 449 us
    all_gather x1 -> x0, waiting for transfers between devices: 51.5 us -> none  [shards(): gathered = lax.all_gather(precond[:, None], OWNER, axis=1, tiled=True)]
    all_to_all x0 -> x1, waiting for transfers between devices: none -> 48.7 us  [shards(): lax.all_to_all(jnp.stack([precond[:, None]] * lax.axis_size(OWNER)), OWNE...]
    reduce_scatter x1, waiting for transfers between devices: 136 us -> 147 us  [shards(): lax.psum_scatter(jnp.einsum('tk,tl->kl', pre_out, mine_in, preferred_elem...]
where the time goes in v1:
time: 592 us
  waiting for transfers between devices  449 us (76%)
  matrix products  43.3 us (7%)
  blocking collectives  43.3 us (7%)
  other arithmetic  21.7 us (4%)
  local copies, waits for them, and re-layouts  14.6 us (2%)
  between operations  13.9 us (2%)
  starting transfers between devices  5.92 us (1%)
    reduce_scatter x1, waiting for transfers between devices, sum_in_two_steps(): lax.psum_scatter(padded_to(lines, lax.axis_size(axis)), axis, scatter_dim...  156 us
    reduce_scatter x1, waiting for transfers between devices, shards(): lax.psum_scatter(jnp.einsum('tk,tl->kl', pre_out, mine_in, preferred_elem...  147 us
    all_gather x1, waiting for transfers between devices, sum_in_two_steps(): whole = lax.all_gather(own, axis).reshape(-1, *lines.shape[1:])  97.3 us
    all_to_all x1, waiting for transfers between devices, shards(): lax.all_to_all(jnp.stack([precond[:, None]] * lax.axis_size(OWNER)), OWNE...  48.7 us
    psum x5, blocking collectives, over_axes(): return functools.reduce(lax.psum, axes, shard)  43.3 us
    dot_general x1, matrix products, shards(): jnp.einsum('skl,slm->skm', product, first_low, preferred_element_type=jnp...  24.7 us
  transfers between devices with their start and end apart: 4, of which 4 were waited for; matrix products, arithmetic and copies ran while one was open for 1% of the time, Pallas kernels for 0%

profile of v1, /device:TPU:8, one launch (start us, length us, event | category | flops | bytes accessed | tf_op | source)
XLA Modules:
  0.0 591.8 jit_solution(17079609428639322440)
XLA Ops:
  6.5 0.0 copy-start.2
  6.5 0.0 reduce-scatter.3.cloned.1.call-start
  6.5 1.6 fusion.10
  8.2 1.6 fusion.12
  9.7 0.0 copy-done.2
  9.8 0.3 fusion.19
  10.1 4.5 fusion.16
  14.6 0.0 reduce-scatter.3.cloned.1.call-update
  14.6 0.0 all-gather.3.cloned.1.call-start
  14.7 156.3 %reduce-scatter.3.cloned.1.call-done = f32[64,1024]{1,0:T(8,128)} async-done(((f32[2048,1024]{1,0:T(8,128)}), f32[64,1024]{1,0:T(8,128)}) %reduce-scatter.3.cloned.1.call-update) | async-done | bytes 262160 | tf_op jit(solution)/shard_map/reduce_scatter | solution.py:24
  170.9 0.0 all-gather.3.cloned.1.call-update
  171.0 2.4 fusion.6
  173.4 2.5 fusion.5
  175.9 97.3 %all-gather.3.cloned.1.call-done = f32[2048,1024]{1,0:T(8,128)} async-done(((f32[64,1024]{1,0:T(8,128)}), f32[2048,1024]{1,0:T(8,128)}) %all-gather.3.cloned.1.call-update) | async-done | bytes 8388624 | tf_op jit(solution)/shard_map/all_gather | solution.py:27
  273.2 0.0 copy-start.1
  273.2 5.4 broadcast_multiply_fusion
  278.7 0.0 copy-start
  278.7 0.0 copy-done.1
  278.7 4.7 add.64
  283.4 1.0 copy-done
  284.4 4.3 abs_reduce_fusion
  288.7 0.1 reduce_max.10
  288.8 0.1 reduce_max.14
  288.9 0.1 reduce_max.18
  289.0 24.7 %fusion.2 = f32[2,1024,1024]{2,1,0:T(8,128)} fusion(f32[2,1024,1024]{2,1,0:T(8,128)} %bitcast.19, f32[1024,1024]{1,0:T(8,128)} %fusion.6, f32[2]{0:T(128)S(1)} %mul.104, f32[1024,1024]{1,0:T(8,128)} %fusion.5, f32[2]{0:T(128)S(1)} %get-tuple-element.5), kind=kOutput, calls=%fused_computation.8 | convolution fusion | flops 8617197568 | bytes 25165840 | tf_op jit(solution)/shard_map/skl,slm->skm/dot_general | solution.py:67
  313.8 9.5 %fusion.13 = bf16[2,128,1024]{2,1,0:T(8,128)(2,1)S(1)} fusion(f32[2,1024,1024]{2,1,0:T(8,128)} %fusion.2, f32[2,1024,1024]{2,1,0:T(8,128)} %bitcast.20, f32[2]{0:T(128)S(1)} %mul.104, f32[1024,1024]{1,0:T(8,128)} %fusion.5, f32[2]{0:T(128)S(1)} %get-tuple-element.5, f32[1024,1024]{1,0:T(8,128)} %fusion.6, bf16[1,128,1024]{2,1,0:T(8,128)(2,1)S(1)} %get-tuple-element.8, ...), kind=kOutput, calls=%fused_computation.25 | convolution fusion | flops 552075264 | bytes 26214416 | tf_op jit(solution)/shard_map/stk,skl->stl/dot_general | solution.py:69
  323.3 2.5 stack.15
  325.8 5.9 all-to-all-start
  331.7 0.0 reduce-scatter.5.cloned.1.call-start
  331.7 48.7 %all-to-all-done = bf16[8,2,1,128,1024]{4,3,1,2,0:T(8,128)(2,1)} async-done(((bf16[8,2,1,128,1024]{4,3,1,2,0:T(8,128)(2,1)}), bf16[8,2,1,128,1024]{4,3,1,2,0:T(8,128)(2,1)}, u32[]{:S(2)}, u32[]{:S(2)}) %all-to-all-start) | async-done | bytes 4194336 | tf_op jit(solution)/shard_map/all_to_all | solution.py:73
  380.5 2.6 copy.13
  383.1 0.1 slice_bitcast_fusion
  383.2 1.1 slice_bitcast_fusion.1
  384.3 0.9 copy.14
  385.2 1.6 copy.15
  386.8 4.5 convolution_convert_fusion
  391.3 0.0 reduce-scatter.5.cloned.1.call-update
  391.3 146.6 %reduce-scatter.5.cloned.1.call-done = bf16[192,512]{1,0:T(8,128)(2,1)} async-done(((bf16[6144,512]{1,0:T(8,128)(2,1)}), bf16[192,512]{1,0:T(8,128)(2,1)}) %reduce-scatter.5.cloned.1.call-update) | async-done | bytes 196624 | tf_op jit(solution)/shard_map/reduce_scatter | solution.py:81
  537.9 1.6 fusion.14
  539.5 16.7 %psum.35 = f32[]{:T(128)} all-reduce(f32[]{:T(128)} %fusion.14), channel_id=1, replica_groups=mesh['dp_0'=8,'dp_1'=2,'dp_2'=2,'owner_0'=2,'owner_1'=4] {'dp_0'}, use_global_device_ids=true, to_apply=%region_7.0 | all-reduce | flops 1 | bytes 8 | tf_op jit(solution)/shard_map/psum | solution.py:32
  556.2 7.1 %psum.36 = f32[]{:T(128)} all-reduce(f32[]{:T(128)} %psum.35), channel_id=1, replica_groups=mesh['dp_0'=8,'dp_1'=2,'dp_2'=2,'owner_0'=2,'owner_1'=4] {'dp_1'}, use_global_device_ids=true, to_apply=%region_8.0 | all-reduce | flops 1 | bytes 8 | tf_op jit(solution)/shard_map/psum | solution.py:32
  563.3 3.1 psum.37
  566.4 5.6 psum.38
  571.9 11.0 %psum.39 = f32[]{:T(128)} all-reduce(f32[]{:T(128)} %psum.38), channel_id=1, replica_groups=mesh['dp_0'=8,'dp_1'=2,'dp_2'=2,'owner_0'=2,'owner_1'=4] {'owner_1'}, use_global_device_ids=true, to_apply=%region_11.12 | all-reduce | flops 1 | bytes 8 | tf_op jit(solution)/shard_map/psum | solution.py:32
  583.6 1.6 fusion.15
  (3 shorter events, 0.0 us)
Async XLA Ops:
  6.5 3.2 copy-start.2
  6.5 164.4 %reduce-scatter.3.cloned.1.call-start = ((), (), s32[]{:S(2)}) async-start(), calls=%async_computation.3 | async-start | bytes 8650752 | tf_op jit(solution)/shard_map/reduce_scatter | solution.py:24
  14.6 258.6 %all-gather.3.cloned.1.call-start = ((), (), s32[]{:S(2)}) async-start(), calls=%async_computation.5 | async-start | bytes 8650752 | tf_op jit(solution)/shard_map/all_gather | solution.py:27
  273.2 5.5 copy-start.1
  278.7 5.7 copy-start
  325.8 54.6 %all-to-all-start = ((bf16[8,2,1,128,1024]{4,3,1,2,0:T(8,128)(2,1)}), bf16[8,2,1,128,1024]{4,3,1,2,0:T(8,128)(2,1)}, u32[]{:S(2)}, u32[]{:S(2)}) async-start(bf16[8,2,1,128,1024]{4,3,1,2,0:T(8,128)(2,1)} %stack.15), calls=%async_computation.1 | async-start | bytes 8388608 | tf_op jit(solution)/shard_map/all_to_all | solution.py:73
  331.7 206.2 %reduce-scatter.5.cloned.1.call-start = ((), (), s32[]{:S(2)}) async-start(), calls=%async_computation.4 | async-start | bytes 6488064 | tf_op jit(solution)/shard_map/reduce_scatter | solution.py:81
Sparse Core Ops, SparseCore 0:
  14.7 156.1 reduce-scatter.2
  173.7 99.4 all-gather.2
  391.4 146.4 reduce-scatter.4
